TPU v7x, 128 devices: a whole 4x4x4 slice. The times are simulated.
128 devices in a mesh: dp: 64 (over x, z, y), rep: 2 (over core).
Axes of the slice: x: 4, y: 4, z: 4, core: 2. Of those that a mesh axis runs over, the one named last changes fastest.
Arguments:
- pooled: bfloat16 [16, 128, 32768], P(None, ('dp', 'rep')), may hold values from -6 to 6
- slot_of_block: int32 [128], replicated, may hold values from 0 to 127, each once
- dense_part: bfloat16 [128, 32768], P(None, ('dp', 'rep')), may hold values from -6 to 6
- labels: int32 [32768], P(('dp', 'rep')), may hold values 0 or 1
- sample_weight: float32 [32768], P(('dp', 'rep')), may hold values from 0.5 to 18, as said below
- proj_wide: bfloat16 [6, 256, 128], replicated, may hold values from -0.375 to 0.375
- proj_mid: bfloat16 [4, 64, 128], replicated, may hold values from -0.75 to 0.75
- proj_narrow: bfloat16 [16, 16, 128], replicated, may hold values from -1.5 to 1.5
- cross_in: bfloat16 [2, 3456, 256], replicated, may hold values from -0.109375 to 0.109375
- cross_out: bfloat16 [2, 256, 3456], replicated, may hold values from -0.375 to 0.375
- cross_bias: float32 [2, 3456], replicated, may hold values from -3 to 3
- head_weight: float32 [3456], replicated, may hold values from -0.24 to 0.24
Outputs:
- pooled_grad: float32 [16, 128, 32768], P(None, ('dp', 'rep'))
- grad_cross_in: float32 [2, 3456, 256], P(None, ('dp', 'rep'))
- grad_cross_out: float32 [2, 256, 3456], P(None, None, ('dp', 'rep'))
- grad_bias: float32 [2, 3456], P(None, ('dp', 'rep'))
Inputs may be any that keep to these rules, and one draw needn't show every extreme that they name: `slot_of_block`: each number of 0 to 127 appears once. `sample_weight`: positive.
All inputs are finite; a program needn't handle non-finite values. No bound on the sum of `labels` on one device may be relied on, other than what follows from the above.
Results may differ from a plain program's by a relative error of at most 0.014.
Values may be sent and summed in bfloat16 or wider, within the bound.
A program may use at most 128 MiB of HBM per device.

v0:
```python
import jax
import jax.numpy as jnp
from jax import lax
from jax.sharding import Mesh
from jax.sharding import PartitionSpec as P

BLOCK_WIDTH = 16
WIDE_TABLES = 6
MID_TABLES = 4
NARROW_TABLES = 16
WIDE_WIDTH = 256
MID_WIDTH = 64
NARROW_WIDTH = 16
PROJECTED = 128
LAYERS = 2
BLOCKS = 128
DP = ("dp_0", "dp_1", "dp_2")
DP_REP = ("dp_0", "dp_1", "dp_2", "rep")


def split_up(shard, dim, devices):
    before, after = (shard.shape[:dim], shard.shape[dim + 1 :])
    return jnp.moveaxis(shard.reshape(*before, devices, -1, *after), dim, 0)


def joined_along(tiles, dim):
    dims = list(tiles.shape[1:])
    dims[dim] *= tiles.shape[0]
    return jnp.moveaxis(tiles, 0, dim).reshape(dims)


def one_exchange(shard, axis, axes, splits, concats):
    sizes = [lax.axis_size(a) for a in axes]
    tiles = split_up(shard, splits[0], sizes[0])
    tiles = jnp.moveaxis(split_up(tiles, splits[1] + 1, sizes[1]), 0, 1)
    inside = tiles.shape[2:]
    tiles = tiles.reshape(-1, *inside)
    tiles = lax.all_to_all(tiles, axis, split_axis=0, concat_axis=0, tiled=True)
    tiles = joined_along(tiles.reshape(*sizes, *inside), concats[0] + 1)
    return joined_along(tiles, concats[1])


def one_axis_at_a_time(shard, axes):
    for axis in axes:
        shard = lax.psum(shard, axis)
    return shard


def own_tiles(shard, axis, dim):
    devices = lax.axis_size(axis)
    tiles = split_up(shard, dim, devices)
    lines = tiles.reshape(devices, -1)
    extent = max(16, -(-lines.shape[1] // 1024) * 8)
    lines = jnp.pad(lines, ((0, 0), (0, extent * 128 - lines.shape[1]))).reshape(-1, 128)
    own = lax.psum_scatter(lines, axis, scatter_dimension=0, tiled=True)
    return own.reshape(-1)[: tiles[0].size].reshape(tiles.shape[1:])


def table_layout():
    first_end = WIDE_TABLES * (WIDE_WIDTH // BLOCK_WIDTH)
    second_end = first_end + MID_TABLES * (MID_WIDTH // BLOCK_WIDTH)
    return (
        (0, first_end, WIDE_TABLES, WIDE_WIDTH),
        (first_end, second_end, MID_TABLES, MID_WIDTH),
        (second_end, BLOCKS, NARROW_TABLES, NARROW_WIDTH),
    )


def project_tables(logical, proj_tables):
    row_count = logical.shape[2]
    outputs = []
    for layout, proj_table in zip(table_layout(), proj_tables):
        block_start, block_end, table_count, table_width = layout
        pieces = logical[:, block_start:block_end].reshape(
            BLOCK_WIDTH, table_count, table_width // BLOCK_WIDTH, row_count
        )
        matrix = proj_table.reshape(table_count, table_width // BLOCK_WIDTH, BLOCK_WIDTH, PROJECTED)
        result = jnp.einsum("tkco,ctkr->tor", matrix, pieces, preferred_element_type=jnp.float32)
        outputs.append(result.reshape(table_count * PROJECTED, row_count))
    return jnp.concatenate(outputs, 0)


def project_back(proj_grad, proj_tables):
    row_count = proj_grad.shape[1]
    outputs = []
    offset = 0
    for layout, proj_table in zip(table_layout(), proj_tables):
        block_start, block_end, table_count, table_width = layout
        piece = proj_grad[offset : offset + table_count * PROJECTED].reshape(
            table_count, PROJECTED, row_count
        )
        offset = offset + table_count * PROJECTED
        matrix = proj_table.reshape(table_count, table_width // BLOCK_WIDTH, BLOCK_WIDTH, PROJECTED)
        result = jnp.einsum("tkco,tor->ctkr", matrix, piece, preferred_element_type=jnp.float32)
        outputs.append(result.reshape(BLOCK_WIDTH, block_end - block_start, row_count))
    return jnp.concatenate(outputs, 1)


def block_step(
    slots,
    dense_part,
    labels,
    sample_weight,
    slot_of_block,
    proj_tables,
    cross_in,
    cross_out,
    cross_bias,
    head_weight,
):
    logical = jnp.take(slots, slot_of_block, axis=1)
    projected = project_tables(logical, proj_tables)
    start = jnp.concatenate([dense_part.astype(jnp.float32), projected], 0).astype(jnp.bfloat16)
    start_full = start.astype(jnp.float32)
    layer_inputs = [start]
    hidden_list = []
    gate_list = []
    current = start
    for layer in range(LAYERS):
        hidden = jnp.einsum(
            "wk,wr->kr", cross_in[layer], current, preferred_element_type=jnp.float32
        ).astype(jnp.bfloat16)
        gate = (
            jnp.einsum("kw,kr->wr", cross_out[layer], hidden, preferred_element_type=jnp.float32)
            + cross_bias[layer][:, None]
        )
        current = (start_full * gate + current.astype(jnp.float32)).astype(jnp.bfloat16)
        hidden_list.append(hidden)
        gate_list.append(gate)
        layer_inputs.append(current)
    logit = jnp.dot(head_weight, current.astype(jnp.float32), precision=lax.Precision.HIGHEST)
    signal = sample_weight * (jax.nn.sigmoid(logit) - labels.astype(jnp.float32))
    upstream = head_weight[:, None] * signal[None, :]
    start_grad = jnp.zeros(start_full.shape, jnp.float32)
    in_terms = [None] * LAYERS
    out_terms = [None] * LAYERS
    bias_terms = [None] * LAYERS
    for layer in reversed(range(LAYERS)):
        gate_grad = start_full * upstream
        bias_terms[layer] = jnp.sum(gate_grad, axis=1)
        gate_low = gate_grad.astype(jnp.bfloat16)
        out_terms[layer] = jnp.einsum(
            "wr,kr->wk", gate_low, hidden_list[layer], preferred_element_type=jnp.float32
        )
        hidden_grad = jnp.einsum(
            "kw,wr->kr", cross_out[layer], gate_low, preferred_element_type=jnp.float32
        ).astype(jnp.bfloat16)
        in_terms[layer] = jnp.einsum(
            "wr,kr->wk", layer_inputs[layer], hidden_grad, preferred_element_type=jnp.float32
        )
        start_grad = start_grad + gate_list[layer] * upstream
        upstream = upstream + jnp.einsum(
            "wk,kr->wr", cross_in[layer], hidden_grad, preferred_element_type=jnp.float32
        )
    start_grad = start_grad + upstream
    proj_grad = start_grad[PROJECTED:].astype(jnp.bfloat16)
    logical_grad = project_back(proj_grad, proj_tables)
    slot_grad = jnp.zeros(logical_grad.shape, jnp.float32).at[:, slot_of_block, :].set(logical_grad)
    return (slot_grad, jnp.stack(in_terms), jnp.stack(out_terms), jnp.stack(bias_terms))


def body(
    pooled,
    slot_of_block,
    dense_part,
    labels,
    sample_weight,
    proj_wide,
    proj_mid,
    proj_narrow,
    cross_in,
    cross_out,
    cross_bias,
    head_weight,
):
    dp_count = lax.axis_size(DP)
    rep_count = lax.axis_size("rep")
    devices = dp_count * rep_count
    row_count = labels.shape[0]
    blocks_here = pooled.shape[1]
    batch_rows = row_count * devices
    layer_count = cross_in.shape[0]
    received = one_exchange(pooled[:, None, None], DP_REP, (DP, "rep"), (4, 4), (1, 2))
    slots = received.reshape(BLOCK_WIDTH, BLOCKS, row_count)
    local_total = jnp.sum(sample_weight)
    total = one_axis_at_a_time(local_total, DP_REP)
    proj_tables = (proj_wide, proj_mid, proj_narrow)
    slot_grad, in_term, out_term, bias_term = block_step(
        slots,
        dense_part,
        labels,
        sample_weight,
        slot_of_block,
        proj_tables,
        cross_in,
        cross_out,
        cross_bias,
        head_weight,
    )
    sectioned_grad = slot_grad.reshape(
        BLOCK_WIDTH, dp_count, rep_count, blocks_here, 1, 1, row_count
    )
    returned = lax.all_to_all(
        lax.all_to_all(
            sectioned_grad.astype(jnp.bfloat16), DP, split_axis=1, concat_axis=4, tiled=True
        ),
        "rep",
        split_axis=2,
        concat_axis=5,
        tiled=True,
    ).astype(sectioned_grad.dtype)
    returned = returned.reshape(BLOCK_WIDTH, blocks_here, batch_rows)
    weight_terms = jnp.concatenate([in_term, out_term], 0)
    weight_sums = own_tiles(weight_terms.astype(jnp.bfloat16), DP_REP, 1).astype(jnp.float32)
    bias_sums = lax.psum_scatter(bias_term, DP_REP, scatter_dimension=1, tiled=True)
    scale = batch_rows / total
    grad_in = weight_sums[:layer_count] * scale
    grad_out = jnp.swapaxes(weight_sums[layer_count:], 1, 2) * scale
    grad_bias = bias_sums * scale
    return (returned * scale, grad_in, grad_out, grad_bias)


def solution(mesh):
    finer = Mesh(mesh.devices.reshape(4, 4, 4, mesh.shape["rep"]), ("dp_0", "dp_1", "dp_2", "rep"))
    return jax.shard_map(
        body,
        mesh=finer,
        in_specs=(
            P(None, DP_REP, None),
            P(),
            P(None, DP_REP),
            P(DP_REP),
            P(DP_REP),
            P(),
            P(),
            P(),
            P(),
            P(),
            P(),
            P(),
        ),
        out_specs=(
            P(None, DP_REP, None),
            P(None, DP_REP, None),
            P(None, None, DP_REP),
            P(None, DP_REP),
        ),
        check_vma=False,
    )
```

profile of v0, /device:TPU:0, one launch (start us, length us, event | category | flops | bytes accessed | tf_op | source)
XLA Modules:
  0.0 294.4 jit_solution(1450464642006116457)
XLA Ops:
  7.2 1.6 copy.94
  9.1 1.6 copy.69
  10.6 11.2 %all-to-all-start = ((bf16[128,16,1,1,1,256]{5,1,4,3,2,0:T(8,128)(2,1)}), bf16[128,16,1,1,1,256]{5,1,4,3,2,0:T(8,128)(2,1)S(1)}, u32[]{:S(2)}, u32[]{:S(2)}) async-start(bf16[128,16,1,1,1,256]{5,1,4,3,2,0:T(8,128)(2,1)} %bitcast.2), calls=%async_computation | async-start | bytes 2097152 | tf_op jit(solution)/shard_map/all_to_all | solution.py:38
  21.9 0.7 copy.73
  22.6 0.6 reshape.183
  23.2 0.7 slice_reduce_fusion
  23.9 17.0 %all-to-all-done = bf16[128,16,1,1,1,256]{5,1,4,3,2,0:T(8,128)(2,1)S(1)} async-done(((bf16[128,16,1,1,1,256]{5,1,4,3,2,0:T(8,128)(2,1)}), bf16[128,16,1,1,1,256]{5,1,4,3,2,0:T(8,128)(2,1)S(1)}, u32[]{:S(2)}, u32[]{:S(2)}) %all-to-all-start) | async-done | bytes 1048608 | tf_op jit(solution)/shard_map/all_to_all | solution.py:38
  40.9 0.6 gather_fusion
  42.4 0.8 copy.76
  44.5 2.3 fusion.37
  47.2 2.5 fusion.8
  49.9 0.6 fusion.43
  50.6 0.7 fusion.1
  51.4 1.7 fusion.13
  53.8 0.7 fusion.46
  54.5 2.1 convolution_convert_fusion
  56.6 1.8 fusion.11
  58.4 0.8 fusion.40
  59.2 1.0 copy-done.3
  60.2 2.0 convolution_convert_fusion.1
  62.2 0.7 convolution_convert_fusion.2
  62.9 3.8 %concatenate.29 = bf16[1,128,27,256]{3,2,1,0:T(8,128)(2,1)} reshape(bf16[3456,256]{1,0:T(8,128)(2,1)} %convolution_convert_fusion) | data formatting | bytes 3538944 | tf_op jit(solution)/shard_map/concatenate | solution.py:213
  66.7 3.8 %concatenate.28 = bf16[1,128,27,256]{3,2,1,0:T(8,128)(2,1)} reshape(bf16[3456,256]{1,0:T(8,128)(2,1)} %convolution_convert_fusion.1) | data formatting | bytes 3538944 | tf_op jit(solution)/shard_map/concatenate | solution.py:213
  70.5 1.6 concatenate.27
  72.1 3.0 %convolution_convert_fusion.3 = bf16[3456,256]{1,0:T(8,128)(2,1)} fusion(bf16[256,256]{1,0:T(8,128)(2,1)S(1)} %fusion.40, bf16[2048,256]{0,1:T(8,128)(2,1)S(1)} %copy.76, bf16[512,256]{0,1:T(8,128)(2,1)} %copy-done.8, bf16[768,256]{0,1:T(8,128)(2,1)} %copy-done.6, bf16[128,256]{0,1:T(8,128)(2,1)S(1)} %copy-done.12), kind=kOutput, calls=%fused_computation.22 | convolution fusion | flops 460947456 | bytes 3670016 | tf_op jit(solution)/shard_map/wr,kr->wk/dot_general | solution.py:148
  75.1 3.9 %concatenate.26 = bf16[1,128,27,256]{3,2,1,0:T(8,128)(2,1)} reshape(bf16[3456,256]{1,0:T(8,128)(2,1)} %convolution_convert_fusion.3) | data formatting | bytes 3538944 | tf_op jit(solution)/shard_map/concatenate | solution.py:213
  79.0 6.7 %maximum_bitcast_fusion = bf16[128,4,27,256]{3,2,0,1:T(8,128)(2,1)} fusion(bf16[1,128,27,256]{3,2,1,0:T(8,128)(2,1)S(1)} %copy-done.2, bf16[1,128,27,256]{3,2,1,0:T(8,128)(2,1)} %concatenate.28, bf16[1,128,27,256]{3,2,1,0:T(8,128)(2,1)} %concatenate.27, bf16[1,128,27,256]{3,2,1,0:T(8,128)(2,1)} %concatenate.26), kind=kLoop, calls=%fused_computation.2 | loop fusion | flops 10616832 | bytes 14155776 | tf_op jit(solution)/shard_map/transpose | solution.py:23
  85.7 8.0 %copy.83 = bf16[128,4,27,256]{3,2,1,0:T(8,128)(2,1)} copy(bf16[128,4,27,256]{3,2,0,1:T(8,128)(2,1)} %maximum_bitcast_fusion) | data formatting | bytes 14155776 | tf_op jit(solution)/shard_map/transpose | solution.py:23
  93.8 12.5 %reshape.162 = bf16[27648,128]{1,0:T(8,128)(2,1)} reshape(bf16[128,4,27,256]{3,2,1,0:T(8,128)(2,1)} %copy.83) | data formatting | bytes 14155776 | tf_op jit(solution)/shard_map/reshape | solution.py:54
  106.3 0.7 copy-done.21
  107.0 5.7 %fusion.4 = bf16[3456,256]{0,1:T(8,128)(2,1)S(1)} fusion(f32[3456,256]{0,1:T(8,128)} %copy-done.3, bf16[256,256]{1,0:T(8,128)(2,1)S(1)} %fusion.40, f32[3456,256]{0,1:T(8,128)} %copy-done.1, f32[3456,256]{0,1:T(8,128)} %get-tuple-element.31, f32[256]{0:T(256)S(1)} %copy-done.21, f32[3456]{0:T(1024)S(1)} %copy-done.14, bf16[2,3456,256]{2,1,0:T(8,128)(2,1)} %param.20), kind=kOutput, calls=%fused_computation.18 | convolution fusion | flops 459177984 | bytes 14301696 | tf_op jit(solution)/shard_map/wk,kr->wr/dot_general | solution.py:152
  114.5 1.5 maximum_bitcast_fusion.1
  116.2 11.9 %scatter_fusion = f32[16,128,256]{2,0,1:T(8,128)S(1)} fusion(f32[16,128,256]{2,0,1:T(8,128)S(1)} %broadcast_in_dim.18, s32[128]{0:T(128)S(1)} %copy-done.23, f32[128,16,256]{2,1,0:T(8,128)} %maximum_bitcast_fusion.1), kind=kCustom, calls=%fused_computation.1 | custom fusion | bytes 6291968 | tf_op jit(solution)/shard_map/scatter | solution.py:158
  128.1 1.1 convert_element_type.89
  129.2 4.9 %all-to-all-start.1 = ((bf16[16,64,2,1,1,1,256]{6,0,2,5,4,3,1:T(8,128)(2,1)}), bf16[16,64,2,1,1,1,256]{6,0,2,5,4,3,1:T(8,128)(2,1)S(1)}, u32[]{:S(2)}, u32[]{:S(2)}) async-start(bf16[16,64,2,1,1,1,256]{6,0,2,5,4,3,1:T(8,128)(2,1)} %bitcast.47), calls=%async_computation.1 | async-start | bytes 2097152 | tf_op jit(solution)/shard_map/all_to_all | solution.py:204
  134.1 16.6 %psum.28 = f32[]{:T(128)} all-reduce(f32[]{:T(128)} %get-tuple-element.28), channel_id=1, replica_groups=mesh['dp_0'=4,'dp_1'=4,'dp_2'=4,'rep'=2] {'dp_0'}, use_global_device_ids=true, to_apply=%region_2.0 | all-reduce | flops 1 | bytes 8 | tf_op jit(solution)/shard_map/psum | solution.py:45
  150.7 11.1 %psum.29 = f32[]{:T(128)} all-reduce(f32[]{:T(128)} %psum.28), channel_id=1, replica_groups=mesh['dp_0'=4,'dp_1'=4,'dp_2'=4,'rep'=2] {'dp_1'}, use_global_device_ids=true, to_apply=%region_3.0 | all-reduce | flops 1 | bytes 8 | tf_op jit(solution)/shard_map/psum | solution.py:45
  161.8 11.0 %psum.30 = f32[]{:T(128)} all-reduce(f32[]{:T(128)} %psum.29), channel_id=1, replica_groups=mesh['dp_0'=4,'dp_1'=4,'dp_2'=4,'rep'=2] {'dp_2'}, use_global_device_ids=true, to_apply=%region_4.0 | all-reduce | flops 1 | bytes 8 | tf_op jit(solution)/shard_map/psum | solution.py:45
  172.9 3.1 %psum.31 = f32[]{:T(128)} all-reduce(f32[]{:T(128)} %psum.30), channel_id=1, replica_groups=mesh['dp_0'=4,'dp_1'=4,'dp_2'=4,'rep'=2] {'rep'}, use_global_device_ids=true, to_apply=%region_5.6 | all-reduce | flops 1 | bytes 8 | tf_op jit(solution)/shard_map/psum | solution.py:45
  176.7 64.0 %all-reduce.1 = f32[2,3456]{1,0:T(2,128)S(1)} all-reduce(f32[2,3456]{1,0:T(2,128)S(1)} %pad_maximum_fusion.2), channel_id=3, replica_groups=mesh['dp_0'=4,'dp_1'=4,'dp_2'=4,'rep'=2] {'dp_0','dp_1','dp_2','rep'}, use_global_device_ids=true, to_apply=%region_9.10.clone | all-reduce | flops 6912 | bytes 55296
  240.7 0.6 dynamic-slice_multiply_fusion
  241.5 4.6 %all_to_all.32 = bf16[16,1,2,1,64,1,256]{6,0,4,5,3,1,2:T(8,128)(2,1)S(1)} all-to-all(bf16[16,1,2,1,64,1,256]{6,0,4,5,3,1,2:T(8,128)(2,1)S(1)} %copy.81), channel_id=1, replica_groups=mesh['dp_0'=4,'dp_1'=4,'dp_2'=4,'rep'=2] {'rep'}, dimensions={2} | all-to-all | bytes 2097152 | tf_op jit(solution)/shard_map/all_to_all | solution.py:203
  246.3 1.6 copy.82
  248.0 4.1 %mul.105 = f32[16,1,32768]{2,1,0:T(1,128)} reshape(f32[16,1,1,1,64,2,1,256]{7,5,4,0,6,3,2,1:T(2,128)S(1)} %copy.82) | data formatting | bytes 4194304 | tf_op jit(solution)/shard_map/mul | solution.py:220
  252.1 33.3 %reduce-scatter.5.cloned.1.call-done = bf16[216,128]{1,0:T(8,128)(2,1)} async-done(((bf16[27648,128]{1,0:T(8,128)(2,1)}), bf16[216,128]{1,0:T(8,128)(2,1)}) %reduce-scatter.5.cloned.1.call-update) | async-done | bytes 55312
  285.4 0.8 convert_element_type.92
  286.2 0.7 copy.85
  286.9 0.7 copy.86
  (88 shorter events, 6.3 us)
Async XLA Ops:
  7.2 36.8 %copy-start = (bf16[6,256,128]{2,1,0:T(8,128)(2,1)S(1)}, bf16[6,256,128]{2,1,0:T(8,128)(2,1)}, u32[]{:S(2)}) copy-start(bf16[6,256,128]{2,1,0:T(8,128)(2,1)} %param.17) | copy-start | bytes 1179652
  8.9 13.0 %copy-start.10 = (bf16[128,256]{1,0:T(8,128)(2,1)S(1)}, bf16[128,256]{1,0:T(8,128)(2,1)}, u32[]{:S(2)}) copy-start(bf16[128,256]{1,0:T(8,128)(2,1)} %param.14) | copy-start | bytes 196612
  8.9 13.7 %copy-start.13 = (f32[3456]{0:T(1024)S(1)}, f32[3456]{0:T(1024)}, u32[]{:S(2)}) copy-start(f32[3456]{0:T(1024)} %param.23) | copy-start | bytes 41476
  8.9 14.3 %copy-start.26 = (s32[128]{0:T(128)S(1)}, s32[128]{0:T(128)}, u32[]{:S(2)}) copy-start(s32[128]{0:T(128)} %param.13) | copy-start | bytes 1540
  8.9 14.3 %copy-start.15 = (f32[2,3456]{1,0:T(2,128)S(1)}, f32[2,3456]{1,0:T(2,128)}, u32[]{:S(2)}) copy-start(f32[2,3456]{1,0:T(2,128)} %param.22) | copy-start | bytes 82948
  10.6 30.3 %all-to-all-start = ((bf16[128,16,1,1,1,256]{5,1,4,3,2,0:T(8,128)(2,1)}), bf16[128,16,1,1,1,256]{5,1,4,3,2,0:T(8,128)(2,1)S(1)}, u32[]{:S(2)}, u32[]{:S(2)}) async-start(bf16[128,16,1,1,1,256]{5,1,4,3,2,0:T(8,128)(2,1)} %bitcast.2), calls=%async_computation | async-start | bytes 2097152 | tf_op jit(solution)/shard_map/all_to_all | solution.py:38
  21.8 20.1 %copy-start.9 = (bf16[16,16,128]{2,1,0:T(8,128)(2,1)S(1)}, bf16[16,16,128]{2,1,0:T(8,128)(2,1)}, u32[]{:S(2)}) copy-start(bf16[16,16,128]{2,1,0:T(8,128)(2,1)} %param.19) | copy-start | bytes 196612
  21.8 263.6 %reduce-scatter.5.cloned.1.call-start = ((), (), s32[]{:S(2)}) async-start(), calls=%async_computation.4 | async-start | bytes 7133184
  23.2 19.2 %copy-start.22 = (s32[128]{0:T(128)}, s32[128]{0:T(128)S(1)}, u32[]{:S(2)}) copy-start(s32[128]{0:T(128)S(1)} %compare_select_fusion) | copy-start | bytes 1540
  41.8 1.4 copy-start.7
  43.5 0.9 copy-start.11
  43.7 15.5 %copy-start.8 = (bf16[512,256]{0,1:T(8,128)(2,1)}, bf16[512,256]{0,1:T(8,128)(2,1)S(1)}, u32[]{:S(2)}) copy-start(bf16[512,256]{0,1:T(8,128)(2,1)S(1)} %copy.75) | copy-start | bytes 786436
  44.5 14.8 %copy-start.6 = (bf16[768,256]{0,1:T(8,128)(2,1)}, bf16[768,256]{0,1:T(8,128)(2,1)S(1)}, u32[]{:S(2)}) copy-start(bf16[768,256]{0,1:T(8,128)(2,1)S(1)} %copy.74) | copy-start | bytes 1179652
  44.5 2.7 copy-start.4
  44.5 2.7 copy-start.18
  47.2 2.7 copy-start.5
  50.5 0.8 copy-start.12
  50.6 0.8 copy-start.19
  51.4 1.8 copy-start.1
  51.4 1.8 copy-start.24
  51.4 1.8 copy-start.25
  51.4 2.4 copy-start.14
  53.8 2.8 copy-start.20
  58.4 1.8 copy-start.3
  75.1 3.9 %copy-start.2 = (bf16[1,128,27,256]{3,2,1,0:T(8,128)(2,1)S(1)}, bf16[1,128,27,256]{3,2,1,0:T(8,128)(2,1)}, u32[]{:S(2)}) copy-start(bf16[1,128,27,256]{3,2,1,0:T(8,128)(2,1)} %concatenate.29) | copy-start | bytes 5308420
  106.3 0.7 copy-start.21
  114.5 1.8 copy-start.23
  128.1 47.8 %copy-start.17 = (f32[3456]{0:T(1024)S(1)}, f32[3456]{0:T(1024)}, u32[]{:S(2)}) copy-start(f32[3456]{0:T(1024)} %get-tuple-element.21) | copy-start | bytes 41476
  128.1 47.8 %copy-start.16 = (f32[3456]{0:T(1024)S(1)}, f32[3456]{0:T(1024)}, u32[]{:S(2)}) copy-start(f32[3456]{0:T(1024)} %get-tuple-element.20) | copy-start | bytes 41476
  129.2 112.2 %all-to-all-start.1 = ((bf16[16,64,2,1,1,1,256]{6,0,2,5,4,3,1:T(8,128)(2,1)}), bf16[16,64,2,1,1,1,256]{6,0,2,5,4,3,1:T(8,128)(2,1)S(1)}, u32[]{:S(2)}, u32[]{:S(2)}) async-start(bf16[16,64,2,1,1,1,256]{6,0,2,5,4,3,1:T(8,128)(2,1)} %bitcast.47), calls=%async_computation.1 | async-start | bytes 2097152 | tf_op jit(solution)/shard_map/all_to_all | solution.py:204
Sparse Core Ops, SparseCore 0:
  106.4 178.8 reduce-scatter.4
where the time goes:
time: 296 us; the launch traced here: 294 us
  blocking collectives  110 us (37%)
  local copies, waits for them, and re-layouts  63.9 us (22%)
  waiting for transfers between devices  50.3 us (17%)
  matrix products  26.4 us (9%)
  starting transfers between devices  16.1 us (5%)
  between operations  15.3 us (5%)
  other arithmetic  12 us (4%)
    unnamed x1, blocking collectives  64 us
    psum x4, blocking collectives, one_axis_at_a_time(): shard = lax.psum(shard, axis)  41.8 us
    unnamed x2, waiting for transfers between devices  33.3 us
    all_to_all x1, waiting for transfers between devices, one_exchange(): tiles = lax.all_to_all(tiles, axis, split_axis=0, concat_axis=0, tiled=True)  17 us
    concatenate x4, local copies, waits for them, and re-layouts, body(): weight_terms = jnp.concatenate([in_term, out_term], 0)  13.1 us
    reshape x1, local copies, waits for them, and re-layouts, own_tiles(): jnp.pad(lines, ((0, 0), (0, extent * 128 - lines.shape[1])))  12.5 us
    scatter x1, local copies, waits for them, and re-layouts, block_step(): jnp.zeros(logical_grad.shape, jnp.float32).at[:, slot_of_block, :]  11.9 us
    all_to_all x1, starting transfers between devices, one_exchange(): tiles = lax.all_to_all(tiles, axis, split_axis=0, concat_axis=0, tiled=True)  11.2 us
  transfers between devices with their start and end apart: 3, of which 2 were waited for; matrix products, arithmetic and copies ran while one was open for 11% of the time, Pallas kernels for 0%

commit v1 on v0

--- a/solution.py
+++ b/solution.py
@@ -42,7 +42,8 @@
 
 def one_axis_at_a_time(shard, axes):
     for axis in axes:
-        shard = lax.psum(shard, axis)
+        blocks = lax.all_gather(shard, axis)
+        shard = jnp.sum(blocks, axis=0)
     return shard
 
 

time: 296 us -> 296 us (level)
  local copies, waits for them, and re-layouts: 63.9 us -> 72.1 us
  blocking collectives: 110 us -> 104 us
  waiting for transfers between devices: 50.3 us -> 45.5 us
    psum x4 -> x0, blocking collectives: 41.8 us -> none  [one_axis_at_a_time(): shard = lax.psum(shard, axis)]
    unnamed x1 -> x5, blocking collectives: 64 us -> 99.5 us
    unnamed x59 -> x79, local copies, waits for them, and re-layouts: 6.85 us -> 15.1 us
    unnamed x2, waiting for transfers between devices: 33.3 us -> 28.4 us
  transfers between devices with their start and end apart: 3 -> 3, of which waited for: 2 -> 2; matrix products, arithmetic and copies ran while one was open for 11% -> 14% of each run, Pallas kernels for 0% -> 0%
where the time goes in v1:
time: 296 us; the launch traced here: 294 us
  blocking collectives  104 us (35%)
  local copies, waits for them, and re-layouts  72.1 us (24%)
  waiting for transfers between devices  45.5 us (15%)
  matrix products  26.4 us (9%)
  starting transfers between devices  16.1 us (5%)
  between operations  15.3 us (5%)
  other arithmetic  14.5 us (5%)
    unnamed x5, blocking collectives  99.5 us
    unnamed x2, waiting for transfers between devices  28.4 us
    all_to_all x1, waiting for transfers between devices, one_exchange(): tiles = lax.all_to_all(tiles, axis, split_axis=0, concat_axis=0, tiled=True)  17 us
    unnamed x79, local copies, waits for them, and re-layouts  15.1 us
    concatenate x4, local copies, waits for them, and re-layouts, body(): weight_terms = jnp.concatenate([in_term, out_term], 0)  13.1 us
    reshape x1, local copies, waits for them, and re-layouts, own_tiles(): jnp.pad(lines, ((0, 0), (0, extent * 128 - lines.shape[1])))  12.5 us
    scatter x1, local copies, waits for them, and re-layouts, block_step(): jnp.zeros(logical_grad.shape, jnp.float32).at[:, slot_of_block, :]  11.9 us
    all_to_all x1, starting transfers between devices, one_exchange(): tiles = lax.all_to_all(tiles, axis, split_axis=0, concat_axis=0, tiled=True)  11.2 us
  transfers between devices with their start and end apart: 3, of which 2 were waited for; matrix products, arithmetic and copies ran while one was open for 14% of the time, Pallas kernels for 0%

profile of v1, /device:TPU:0, one launch (start us, length us, event | category | flops | bytes accessed | tf_op | source)
XLA Modules:
  0.0 294.0 jit_solution(14252410114949591150)
XLA Ops:
  7.2 1.6 copy.94
  9.1 1.6 copy.69
  10.6 11.2 %all-to-all-start = ((bf16[128,16,1,1,1,256]{5,1,4,3,2,0:T(8,128)(2,1)}), bf16[128,16,1,1,1,256]{5,1,4,3,2,0:T(8,128)(2,1)S(1)}, u32[]{:S(2)}, u32[]{:S(2)}) async-start(bf16[128,16,1,1,1,256]{5,1,4,3,2,0:T(8,128)(2,1)} %bitcast.2), calls=%async_computation | async-start | bytes 2097152 | tf_op jit(solution)/shard_map/all_to_all | solution.py:38
  21.9 0.7 copy.73
  23.2 0.7 slice_reduce_fusion
  23.9 17.0 %all-to-all-done = bf16[128,16,1,1,1,256]{5,1,4,3,2,0:T(8,128)(2,1)S(1)} async-done(((bf16[128,16,1,1,1,256]{5,1,4,3,2,0:T(8,128)(2,1)}), bf16[128,16,1,1,1,256]{5,1,4,3,2,0:T(8,128)(2,1)S(1)}, u32[]{:S(2)}, u32[]{:S(2)}) %all-to-all-start) | async-done | bytes 1048608 | tf_op jit(solution)/shard_map/all_to_all | solution.py:38
  42.4 0.8 copy.76
  44.5 2.3 fusion.37
  47.2 2.5 fusion.8
  51.4 1.7 fusion.13
  53.2 0.7 fusion.56
  53.9 0.7 fusion.46
  54.6 2.0 convolution_convert_fusion
  56.7 1.8 fusion.11
  58.4 0.8 fusion.40
  59.3 0.9 copy-done.3
  60.3 2.0 convolution_convert_fusion.1
  62.3 0.7 convolution_convert_fusion.2
  63.0 3.8 %concatenate.29 = bf16[1,128,27,256]{3,2,1,0:T(8,128)(2,1)} reshape(bf16[3456,256]{1,0:T(8,128)(2,1)} %convolution_convert_fusion) | data formatting | bytes 3538944 | tf_op jit(solution)/shard_map/concatenate | solution.py:214
  66.8 3.8 %concatenate.28 = bf16[1,128,27,256]{3,2,1,0:T(8,128)(2,1)} reshape(bf16[3456,256]{1,0:T(8,128)(2,1)} %convolution_convert_fusion.1) | data formatting | bytes 3538944 | tf_op jit(solution)/shard_map/concatenate | solution.py:214
  70.6 1.6 concatenate.27
  72.2 3.0 %convolution_convert_fusion.3 = bf16[3456,256]{1,0:T(8,128)(2,1)} fusion(bf16[256,256]{1,0:T(8,128)(2,1)S(1)} %fusion.40, bf16[2048,256]{0,1:T(8,128)(2,1)S(1)} %copy.76, bf16[512,256]{0,1:T(8,128)(2,1)} %copy-done.8, bf16[768,256]{0,1:T(8,128)(2,1)} %copy-done.6, bf16[128,256]{0,1:T(8,128)(2,1)S(1)} %copy-done.12), kind=kOutput, calls=%fused_computation.22 | convolution fusion | flops 460947456 | bytes 3670016 | tf_op jit(solution)/shard_map/wr,kr->wk/dot_general | solution.py:149
  75.2 3.9 %concatenate.26 = bf16[1,128,27,256]{3,2,1,0:T(8,128)(2,1)} reshape(bf16[3456,256]{1,0:T(8,128)(2,1)} %convolution_convert_fusion.3) | data formatting | bytes 3538944 | tf_op jit(solution)/shard_map/concatenate | solution.py:214
  79.1 6.7 %maximum_bitcast_fusion = bf16[128,4,27,256]{3,2,0,1:T(8,128)(2,1)} fusion(bf16[1,128,27,256]{3,2,1,0:T(8,128)(2,1)S(1)} %copy-done.2, bf16[1,128,27,256]{3,2,1,0:T(8,128)(2,1)} %concatenate.28, bf16[1,128,27,256]{3,2,1,0:T(8,128)(2,1)} %concatenate.27, bf16[1,128,27,256]{3,2,1,0:T(8,128)(2,1)} %concatenate.26), kind=kLoop, calls=%fused_computation.2 | loop fusion | flops 10616832 | bytes 14155776 | tf_op jit(solution)/shard_map/transpose | solution.py:23
  85.8 8.0 %copy.83 = bf16[128,4,27,256]{3,2,1,0:T(8,128)(2,1)} copy(bf16[128,4,27,256]{3,2,0,1:T(8,128)(2,1)} %maximum_bitcast_fusion) | data formatting | bytes 14155776 | tf_op jit(solution)/shard_map/transpose | solution.py:23
  93.8 12.5 %reshape.162 = bf16[27648,128]{1,0:T(8,128)(2,1)} reshape(bf16[128,4,27,256]{3,2,1,0:T(8,128)(2,1)} %copy.83) | data formatting | bytes 14155776 | tf_op jit(solution)/shard_map/reshape | solution.py:55
  107.0 5.7 %fusion.4 = bf16[3456,256]{0,1:T(8,128)(2,1)S(1)} fusion(f32[3456,256]{0,1:T(8,128)} %copy-done.3, bf16[256,256]{1,0:T(8,128)(2,1)S(1)} %fusion.40, f32[3456,256]{0,1:T(8,128)} %copy-done.1, f32[3456,256]{0,1:T(8,128)} %get-tuple-element.31, f32[256]{0:T(256)S(1)} %copy-done.21, f32[3456]{0:T(1024)S(1)} %copy-done.14, bf16[2,3456,256]{2,1,0:T(8,128)(2,1)} %param.20), kind=kOutput, calls=%fused_computation.18 | convolution fusion | flops 459177984 | bytes 14301696 | tf_op jit(solution)/shard_map/wk,kr->wr/dot_general | solution.py:153
  114.5 1.5 maximum_bitcast_fusion.1
  116.3 11.9 %scatter_fusion = f32[16,128,256]{2,0,1:T(8,128)S(1)} fusion(f32[16,128,256]{2,0,1:T(8,128)S(1)} %broadcast_in_dim.18, s32[128]{0:T(128)S(1)} %copy-done.23, f32[128,16,256]{2,1,0:T(8,128)} %maximum_bitcast_fusion.1), kind=kCustom, calls=%fused_computation.1 | custom fusion | bytes 6291968 | tf_op jit(solution)/shard_map/scatter | solution.py:159
  128.2 1.1 convert_element_type.89
  129.3 4.9 %all-to-all-start.1 = ((bf16[16,64,2,1,1,1,256]{6,0,2,5,4,3,1:T(8,128)(2,1)}), bf16[16,64,2,1,1,1,256]{6,0,2,5,4,3,1:T(8,128)(2,1)S(1)}, u32[]{:S(2)}, u32[]{:S(2)}) async-start(bf16[16,64,2,1,1,1,256]{6,0,2,5,4,3,1:T(8,128)(2,1)} %bitcast.47), calls=%async_computation.1 | async-start | bytes 2097152 | tf_op jit(solution)/shard_map/all_to_all | solution.py:205
  134.9 0.7 dynamic-slice.1
  136.2 1.4 dynamic-update-slice
  138.2 12.1 %all-reduce = f32[4]{0:T(128)S(1)} all-reduce(f32[4]{0:T(128)S(1)} %dynamic-update-slice), channel_id=1, replica_groups=mesh['dp_0'=4,'dp_1'=4,'dp_2'=4,'rep'=2] {'dp_0'}, use_global_device_ids=true, to_apply=%add | all-reduce | flops 4 | bytes 32
  151.0 1.4 dynamic-update-slice.1
  152.4 10.5 %all-reduce.1 = f32[4]{0:T(128)S(1)} all-reduce(f32[4]{0:T(128)S(1)} %dynamic-update-slice.1), channel_id=1, replica_groups=mesh['dp_0'=4,'dp_1'=4,'dp_2'=4,'rep'=2] {'dp_1'}, use_global_device_ids=true, to_apply=%add.1 | all-reduce | flops 4 | bytes 32
  163.5 1.4 dynamic-update-slice.2
  164.9 10.4 %all-reduce.2 = f32[4]{0:T(128)S(1)} all-reduce(f32[4]{0:T(128)S(1)} %dynamic-update-slice.2), channel_id=1, replica_groups=mesh['dp_0'=4,'dp_1'=4,'dp_2'=4,'rep'=2] {'dp_2'}, use_global_device_ids=true, to_apply=%add.2 | all-reduce | flops 4 | bytes 32
  175.9 1.4 dynamic-update-slice.3
  177.3 2.4 all-reduce.3
  181.1 64.1 %all-reduce.5 = f32[2,3456]{1,0:T(2,128)S(1)} all-reduce(f32[2,3456]{1,0:T(2,128)S(1)} %pad_maximum_fusion.2), channel_id=3, replica_groups=mesh['dp_0'=4,'dp_1'=4,'dp_2'=4,'rep'=2] {'dp_0','dp_1','dp_2','rep'}, use_global_device_ids=true, to_apply=%region_9.10.clone | all-reduce | flops 6912 | bytes 55296
  245.9 4.6 %all_to_all.32 = bf16[16,1,2,1,64,1,256]{6,0,4,5,3,1,2:T(8,128)(2,1)S(1)} all-to-all(bf16[16,1,2,1,64,1,256]{6,0,4,5,3,1,2:T(8,128)(2,1)S(1)} %copy.81), channel_id=1, replica_groups=mesh['dp_0'=4,'dp_1'=4,'dp_2'=4,'rep'=2] {'rep'}, dimensions={2} | all-to-all | bytes 2097152 | tf_op jit(solution)/shard_map/all_to_all | solution.py:204
  250.8 1.6 copy.82
  252.4 4.1 %mul.105 = f32[16,1,32768]{2,1,0:T(1,128)} reshape(f32[16,1,1,1,64,2,1,256]{7,5,4,0,6,3,2,1:T(2,128)S(1)} %copy.82) | data formatting | bytes 4194304 | tf_op jit(solution)/shard_map/mul | solution.py:221
  256.5 28.4 %reduce-scatter.5.cloned.1.call-done = bf16[216,128]{1,0:T(8,128)(2,1)} async-done(((bf16[27648,128]{1,0:T(8,128)(2,1)}), bf16[216,128]{1,0:T(8,128)(2,1)}) %reduce-scatter.5.cloned.1.call-update) | async-done | bytes 55312
  284.9 0.8 convert_element_type.92
  285.8 0.7 copy.85
  286.5 0.7 copy.86
  (112 shorter events, 13.8 us)
Async XLA Ops:
  7.2 36.8 %copy-start = (bf16[6,256,128]{2,1,0:T(8,128)(2,1)S(1)}, bf16[6,256,128]{2,1,0:T(8,128)(2,1)}, u32[]{:S(2)}) copy-start(bf16[6,256,128]{2,1,0:T(8,128)(2,1)} %param.17) | copy-start | bytes 1179652
  8.9 13.0 %copy-start.10 = (bf16[128,256]{1,0:T(8,128)(2,1)S(1)}, bf16[128,256]{1,0:T(8,128)(2,1)}, u32[]{:S(2)}) copy-start(bf16[128,256]{1,0:T(8,128)(2,1)} %param.14) | copy-start | bytes 196612
  8.9 13.7 %copy-start.13 = (f32[3456]{0:T(1024)S(1)}, f32[3456]{0:T(1024)}, u32[]{:S(2)}) copy-start(f32[3456]{0:T(1024)} %param.23) | copy-start | bytes 41476
  8.9 14.3 %copy-start.26 = (s32[128]{0:T(128)S(1)}, s32[128]{0:T(128)}, u32[]{:S(2)}) copy-start(s32[128]{0:T(128)} %param.13) | copy-start | bytes 1540
  8.9 14.3 %copy-start.15 = (f32[2,3456]{1,0:T(2,128)S(1)}, f32[2,3456]{1,0:T(2,128)}, u32[]{:S(2)}) copy-start(f32[2,3456]{1,0:T(2,128)} %param.22) | copy-start | bytes 82948
  10.6 30.3 %all-to-all-start = ((bf16[128,16,1,1,1,256]{5,1,4,3,2,0:T(8,128)(2,1)}), bf16[128,16,1,1,1,256]{5,1,4,3,2,0:T(8,128)(2,1)S(1)}, u32[]{:S(2)}, u32[]{:S(2)}) async-start(bf16[128,16,1,1,1,256]{5,1,4,3,2,0:T(8,128)(2,1)} %bitcast.2), calls=%async_computation | async-start | bytes 2097152 | tf_op jit(solution)/shard_map/all_to_all | solution.py:38
  21.8 20.1 %copy-start.9 = (bf16[16,16,128]{2,1,0:T(8,128)(2,1)S(1)}, bf16[16,16,128]{2,1,0:T(8,128)(2,1)}, u32[]{:S(2)}) copy-start(bf16[16,16,128]{2,1,0:T(8,128)(2,1)} %param.19) | copy-start | bytes 196612
  21.8 263.1 %reduce-scatter.5.cloned.1.call-start = ((), (), s32[]{:S(2)}) async-start(), calls=%async_computation.4 | async-start | bytes 7133184
  23.2 19.2 %copy-start.22 = (s32[128]{0:T(128)}, s32[128]{0:T(128)S(1)}, u32[]{:S(2)}) copy-start(s32[128]{0:T(128)S(1)} %compare_select_fusion) | copy-start | bytes 1540
  41.8 1.4 copy-start.7
  43.5 0.9 copy-start.11
  43.7 15.6 %copy-start.8 = (bf16[512,256]{0,1:T(8,128)(2,1)}, bf16[512,256]{0,1:T(8,128)(2,1)S(1)}, u32[]{:S(2)}) copy-start(bf16[512,256]{0,1:T(8,128)(2,1)S(1)} %copy.75) | copy-start | bytes 786436
  44.5 14.8 %copy-start.6 = (bf16[768,256]{0,1:T(8,128)(2,1)}, bf16[768,256]{0,1:T(8,128)(2,1)S(1)}, u32[]{:S(2)}) copy-start(bf16[768,256]{0,1:T(8,128)(2,1)S(1)} %copy.74) | copy-start | bytes 1179652
  44.5 2.7 copy-start.4
  44.5 2.7 copy-start.18
  47.2 2.7 copy-start.5
  50.5 0.8 copy-start.12
  50.6 0.8 copy-start.19
  51.4 1.8 copy-start.1
  51.4 1.8 copy-start.24
  51.4 1.8 copy-start.25
  51.4 2.5 copy-start.14
  53.9 2.8 copy-start.20
  58.4 1.8 copy-start.3
  75.2 3.9 %copy-start.2 = (bf16[1,128,27,256]{3,2,1,0:T(8,128)(2,1)S(1)}, bf16[1,128,27,256]{3,2,1,0:T(8,128)(2,1)}, u32[]{:S(2)}) copy-start(bf16[1,128,27,256]{3,2,1,0:T(8,128)(2,1)} %concatenate.29) | copy-start | bytes 5308420
  106.4 0.7 copy-start.21
  114.5 1.8 copy-start.23
  128.2 6.1 %copy-start.30 = (u32[128]{0:T(128)S(1)}, u32[128]{0:T(128)}, u32[]{:S(2)}) copy-start(u32[128]{0:T(128)} %constant.29) | copy-start | bytes 1540
  128.2 6.7 %copy-start.29 = (u32[128]{0:T(128)S(1)}, u32[128]{0:T(128)}, u32[]{:S(2)}) copy-start(u32[128]{0:T(128)} %constant.34) | copy-start | bytes 1540
  128.2 7.3 %copy-start.28 = (u32[128]{0:T(128)S(1)}, u32[128]{0:T(128)}, u32[]{:S(2)}) copy-start(u32[128]{0:T(128)} %constant.39) | copy-start | bytes 1540
  128.2 9.4 %copy-start.27 = (u32[128]{0:T(128)S(1)}, u32[128]{0:T(128)}, u32[]{:S(2)}) copy-start(u32[128]{0:T(128)} %constant.44) | copy-start | bytes 1540
  128.2 51.5 %copy-start.17 = (f32[3456]{0:T(1024)S(1)}, f32[3456]{0:T(1024)}, u32[]{:S(2)}) copy-start(f32[3456]{0:T(1024)} %get-tuple-element.21) | copy-start | bytes 41476
  128.2 51.5 %copy-start.16 = (f32[3456]{0:T(1024)S(1)}, f32[3456]{0:T(1024)}, u32[]{:S(2)}) copy-start(f32[3456]{0:T(1024)} %get-tuple-element.20) | copy-start | bytes 41476
  129.3 116.5 %all-to-all-start.1 = ((bf16[16,64,2,1,1,1,256]{6,0,2,5,4,3,1:T(8,128)(2,1)}), bf16[16,64,2,1,1,1,256]{6,0,2,5,4,3,1:T(8,128)(2,1)S(1)}, u32[]{:S(2)}, u32[]{:S(2)}) async-start(bf16[16,64,2,1,1,1,256]{6,0,2,5,4,3,1:T(8,128)(2,1)} %bitcast.47), calls=%async_computation.1 | async-start | bytes 2097152 | tf_op jit(solution)/shard_map/all_to_all | solution.py:205
Sparse Core Ops, SparseCore 0:
  106.5 178.3 reduce-scatter.4
